TPU v7x, 128 devices: a whole 4x4x4 slice. The times are simulated.
128 devices in a mesh: scan: 16 (over z, y), row: 8 (over x, core).
Axes of the slice: x: 4, y: 4, z: 4, core: 2. Of those that a mesh axis runs over, the one named last changes fastest.
Arguments:
- raw_planes: float32 [32, 6, 128, 1024], P('scan', None, 'row'), may hold values from 0 to 4
- shear_tiles: int32 [32], P('scan'), may hold values from 0 to 5, as said below
- axial_kernel: float32 [64], replicated, may hold values from 0.05 to 1
- column_kernel: float32 [31], replicated, may hold values from 0.05 to 1
- row_kernel: float32 [31], replicated, may hold values from 0.05 to 1
Outputs:
- estimate: float32 [32, 16, 128, 1024], P(None, 'scan', 'row')
Inputs may be any that keep to these rules, and one draw needn't show every extreme that they name: `shear_tiles`: plane p has a shear within one tile of p * 5 // 31; the first plane has 0 and the last 5.
All inputs are finite; a program needn't handle non-finite values.
Results may differ from a plain program's by a relative error of at most 0.0003.
Values sent between devices are 32-bit elements; how exact they have to be, the bound alone decides.
A program may use at most 128 MiB of HBM per device.

v0:
```python
import jax
import jax.numpy as jnp
from jax import lax
from jax.sharding import PartitionSpec as P

TILES_DEV = 1
ITERS = 2
background_level = 0.5


def normalized(kernel):
    return kernel / jnp.sum(kernel)


def band_matrix(kernel, extent):
    length = kernel.shape[0]
    centre = length // 2
    indices = jnp.arange(extent, dtype=jnp.int32)
    offset = indices[None, :] - indices[:, None] + centre
    inside = (offset >= 0) & (offset < length)
    return jnp.where(inside, kernel[jnp.clip(offset, 0, length - 1)], 0.0)


def shifted_sum(volume, kernel, centre, axis):
    length = kernel.shape[0]
    extent = volume.shape[axis]
    widths = [(0, 0)] * volume.ndim
    widths[axis] = (centre, length - 1 - centre)
    padded = jnp.pad(volume, widths)
    summed = jnp.zeros_like(volume)
    for tap in range(length):
        summed = summed + kernel[tap] * lax.slice_in_dim(padded, tap, tap + extent, axis=axis)
    return summed


def spread_planes(tiles_in, shear_tiles, total):

    def place_plane(one_plane, offset):
        empty_slab = jnp.zeros((total,) + one_plane.shape[1:], one_plane.dtype)
        anchor = jnp.zeros((), jnp.int32)
        return lax.dynamic_update_slice(empty_slab, one_plane, (offset, anchor, anchor))

    return jax.vmap(place_plane)(tiles_in, shear_tiles)


def axial_apply(matrix, volume):
    flattened = volume.reshape(volume.shape[0], -1)
    result = jnp.dot(matrix, flattened, precision=lax.Precision.HIGHEST)
    return result.reshape(volume.shape)


def rows_layout(volume):
    result = lax.all_to_all(
        lax.all_to_all(volume, "scan", split_axis=0, concat_axis=1, tiled=True),
        "row",
        split_axis=3,
        concat_axis=2,
        tiled=True,
    )
    return result


def pencil_layout(volume):
    result = lax.all_to_all(
        lax.all_to_all(volume, "scan", split_axis=1, concat_axis=0, tiled=True),
        "row",
        split_axis=2,
        concat_axis=3,
        tiled=True,
    )
    return result


def shards(raw_planes, shear_tiles, axial_kernel, column_kernel, row_kernel):
    scan_count = lax.axis_size("scan")
    out_count = TILES_DEV * scan_count
    axial = normalized(axial_kernel)
    across = normalized(column_kernel)
    down = normalized(row_kernel)
    lateral_len = across.shape[0]
    lateral_centre = lateral_len // 2
    back_centre = lateral_len - 1 - lateral_centre
    spread = spread_planes(raw_planes, shear_tiles, out_count)
    data_pencils = lax.all_to_all(spread, "scan", split_axis=1, concat_axis=0, tiled=True)
    data_rows = rows_layout(data_pencils)
    row_shape = data_rows.shape
    data_flat = data_rows.reshape(row_shape[0], row_shape[1] * row_shape[2], row_shape[3])
    axial_band = band_matrix(axial, data_pencils.shape[0])
    estimate = data_pencils + 1.0
    for iteration in range(ITERS):
        blurred = axial_apply(axial_band, estimate)
        blurred = shifted_sum(blurred, across, lateral_centre, 3)
        blurred_rows = rows_layout(blurred)
        flattened = blurred_rows.reshape(data_flat.shape)
        flattened = shifted_sum(flattened, down, lateral_centre, 1)
        quotient = data_flat / (flattened + background_level)
        quotient = shifted_sum(quotient, down[::-1], back_centre, 1)
        correction = pencil_layout(quotient.reshape(row_shape))
        correction = shifted_sum(correction, across[::-1], back_centre, 3)
        correction = axial_apply(axial_band.T, correction)
        estimate = estimate * correction
    return estimate


def solution(mesh):
    return jax.shard_map(
        shards,
        mesh=mesh,
        in_specs=(P("scan", None, "row", None), P("scan"), P(), P(), P()),
        out_specs=P(None, "scan", "row", None),
        check_vma=False,
    )
```

profile of v0, /device:TPU:1, one launch (start us, length us, event | category | flops | bytes accessed | tf_op | source)
XLA Modules:
  0.0 926.5 jit_solution(2786880016588994488)
XLA Ops:
  0.0 0.7 fusion.324
  1.6 1.6 broadcast_in_dim.16.clone
  3.2 17.7 %while.1 = (s32[]{:T(128)}, f32[2,16,16,1024]{3,2,0,1:T(8,128)}, s32[2,4]{1,0:T(2,128)S(1)}, f32[2,6,16,1024]{3,2,1,0:T(8,128)S(1)}, s32[]{:T(128)}, /*index=5*/s32[4]{0:T(128)S(1)}) while((s32[]{:T(128)}, f32[2,16,16,1024]{3,2,0,1:T(8,128)}, s32[2,4]{1,0:T(2,128)S(1)}, f32[2,6,16,1024]{3,2,1,0:T(8,128)S(1)}, s32[]{:T(128)}, ...), condition=%wide.while_cond, body=%wide.while_body.sunk | while | flops 98333 | bytes 1968306 | solution.py:41
  3.8 3.2 and_reduce_fusion.2
  7.0 2.3 constant_dynamic-slice_fusion.5
  9.3 2.7 bitcast_dynamic-update-slice_fusion.2
  12.6 3.2 and_reduce_fusion.2
  15.8 2.3 constant_dynamic-slice_fusion.5
  18.1 2.7 bitcast_dynamic-update-slice_fusion.2
  20.8 8.8 all-to-all-start
  31.7 6.6 gather_fusion
  40.5 19.7 %all-to-all-done = f32[2,16,16,1024]{3,2,0,1:T(8,128)} async-done(((f32[2,16,16,1024]{3,2,0,1:T(8,128)}), f32[2,16,16,1024]{3,2,0,1:T(8,128)}, u32[]{:S(2)}, u32[]{:S(2)}) %all-to-all-start) | async-done | bytes 2097184 | tf_op jit(solution)/shard_map/all_to_all | solution.py:84
  60.2 1.8 bitcast_add_fusion
  61.9 1.2 copy.151
  63.2 1.9 fusion.329
  65.2 1.2 copy.152
  66.4 36.0 %fusion.53 = f32[32,1,16,1024]{3,2,1,0:T(8,128)S(1)} fusion(f32[32,1,16,1024]{3,2,1,0:T(8,128)S(1)} %bitcast.299, f32[]{:T(128)} %bitcast.50, f32[]{:T(128)} %bitcast.49, f32[]{:T(128)} %bitcast.48, f32[]{:T(128)} %bitcast.47, f32[]{:T(128)} %bitcast.46, f32[]{:T(128)} %bitcast.45, f32[]{:T(128)} %bitcast.44, f32[]{:T(128)} %bitcast.43, f32[]{:T(128)} %bitcast.42, ...), kind=kLoop, calls=%fused_computation.179 | loop fusion | flops 31981568 | bytes 4194428 | tf_op jit(solution)/shard_map/add | solution.py:32
  102.4 31.3 %all_to_all.189 = f32[32,1,16,1024]{3,2,1,0:T(8,128)} all-to-all(f32[32,1,16,1024]{3,2,1,0:T(8,128)S(1)} %fusion.53), channel_id=1, replica_groups=mesh['scan'=16,'row'=8] {'scan'}, dimensions={0} | all-to-all | bytes 4194304 | tf_op jit(solution)/shard_map/all_to_all | solution.py:54
  133.6 4.1 all-to-all-start.1
  137.7 21.4 %copy.97 = f32[2,16,16,1024]{2,0,1,3:T(2,128)} copy(f32[2,16,16,1024]{3,2,0,1:T(8,128)} %bitcast.293) | data formatting | bytes 4194304 | tf_op jit(solution)/shard_map/all_to_all | solution.py:54
  159.1 24.7 %reshape.188 = f32[8,1,65536]{2,1,0:T(1,128)} reshape(f32[1024,16,2,16]{3,2,1,0:T(2,128)} %bitcast.282) | data formatting | bytes 4194304
  183.9 6.6 all-to-all-start.4
  190.4 13.6 %copy.92 = f32[16,2,1,16,1024]{3,0,1,4,2:T(8,128)} copy(f32[16,2,1,16,1024]{4,3,1,0,2:T(8,128)S(1)} %bitcast.292) | data formatting | bytes 4194304 | tf_op jit(solution)/shard_map/all_to_all | solution.py:54
  204.0 11.6 %bitcast_bitcast_fusion = f32[1024,2,16,16]{3,2,1,0:T(8,128)} fusion(f32[16,2,1,16,1024]{3,0,1,4,2:T(8,128)} %copy.92), kind=kLoop, calls=%fused_computation.512 | loop fusion | bytes 4194304
  215.6 11.6 %reshape.186 = f32[8,1,65536]{2,1,0:T(1,128)} reshape(f32[1024,2,16,16]{3,2,1,0:T(8,128)} %bitcast_bitcast_fusion) | data formatting | bytes 4194304
  227.2 4.9 all-to-all-start.2
  234.9 0.7 fusion.336
  236.9 7.3 reduce.3
  244.2 28.4 %reshape.189 = f32[1024,16,2,16]{3,2,1,0:T(2,128)} reshape(f32[8,65536]{1,0:T(8,128)S(1)} %reduce.3) | data formatting | bytes 4194304
  272.6 21.8 %copy.130 = f32[2,16,16,8,128]{4,2,3,1,0:T(8,128)} copy(f32[2,16,16,8,128]{2,0,1,4,3:T(2,128)} %bitcast.283) | data formatting | bytes 4194304 | tf_op jit(solution)/shard_map/all_to_all | solution.py:53
  294.5 7.3 reduce.2
  301.7 11.3 %reshape.187 = f32[1024,2,16,16]{3,2,1,0:T(8,128)} reshape(f32[8,65536]{1,0:T(8,128)S(1)} %reduce.2) | data formatting | bytes 4194304
  313.0 9.8 %copy.94 = f32[2,16,8,16,128]{4,3,2,1,0:T(8,128)S(1)} copy(f32[2,16,8,16,128]{3,1,0,4,2:T(8,128)} %bitcast.284) | data formatting | bytes 4194304 | tf_op jit(solution)/shard_map/all_to_all | solution.py:53
  322.8 57.8 %bitcast_divide_fusion.1 = f32[2,2048,128]{2,1,0:T(8,128)S(1)} fusion(f32[2,16,8,16,128]{4,3,2,1,0:T(8,128)S(1)} %copy.94, f32[2,2048,128]{2,1,0:T(8,128)} %bitcast.291, f32[]{:T(128)} %bitcast.88, f32[]{:T(128)} %bitcast.87, f32[]{:T(128)} %bitcast.86, f32[]{:T(128)} %bitcast.85, f32[]{:T(128)} %bitcast.84, f32[]{:T(128)} %bitcast.83, f32[]{:T(128)} %bitcast.82, ...), kind=kLoop, calls=%fused_computation.373 | loop fusion | flops 33030144 | bytes 6291580 | tf_op jit(solution)/shard_map/div | solution.py:96
  380.6 27.4 %multiply_add_fusion.1 = f32[2,2048,128]{2,1,0:T(8,128)S(1)} fusion(f32[2,2048,128]{2,1,0:T(8,128)S(1)} %bitcast_divide_fusion.1, f32[]{:T(128)} %bitcast.118, f32[]{:T(128)} %bitcast.117, f32[]{:T(128)} %bitcast.116, f32[]{:T(128)} %bitcast.115, f32[]{:T(128)} %bitcast.114, f32[]{:T(128)} %bitcast.113, f32[]{:T(128)} %bitcast.112, f32[]{:T(128)} %bitcast.111, ...), kind=kLoop, calls=%fused_computation.430 | loop fusion | flops 31981568 | bytes 4194428 | tf_op jit(solution)/shard_map/add | solution.py:32
  408.3 34.8 %all_to_all.190 = f32[2,16,128,128]{3,2,0,1:T(8,128)S(1)} all-to-all(f32[2,16,128,128]{3,2,0,1:T(8,128)S(1)} %copy.100), channel_id=1, replica_groups=mesh['scan'=16,'row'=8] {'scan'}, dimensions={1} | all-to-all | bytes 4194304 | tf_op jit(solution)/shard_map/all_to_all | solution.py:65
  443.1 2.5 copy.101
  445.6 5.7 all-to-all-start.6
  452.8 25.0 %all-to-all-done.6 = f32[32,1,128,128]{3,0,1,2:T(8,128)} async-done(((f32[32,1,128,128]{3,0,1,2:T(8,128)}), f32[32,1,128,128]{3,0,1,2:T(8,128)}, u32[]{:S(2)}, u32[]{:S(2)}) %all-to-all-start.6) | async-done | bytes 2097184 | tf_op jit(solution)/shard_map/all_to_all | solution.py:64
  477.8 2.8 copy.102
  480.6 0.9 copy.103
  482.0 36.3 %fusion.113 = f32[32,1,16,1024]{3,2,1,0:T(8,128)S(1)} fusion(f32[32,1,16,1024]{3,2,1,0:T(8,128)S(1)} %copy.104, f32[]{:T(128)} %bitcast.155, f32[]{:T(128)} %bitcast.154, f32[]{:T(128)} %bitcast.153, f32[]{:T(128)} %bitcast.152, f32[]{:T(128)} %bitcast.151, f32[]{:T(128)} %bitcast.150, f32[]{:T(128)} %bitcast.149, f32[]{:T(128)} %bitcast.148, f32[]{:T(128)} %bitcast.147, ...), kind=kLoop, calls=%fused_computation.239 | loop fusion | flops 31981568 | bytes 4194428 | tf_op jit(solution)/shard_map/add | solution.py:32
  518.3 4.1 copy_multiply_fusion
  522.7 1.1 copy-done
  523.8 1.9 fusion.326
  525.7 1.2 copy.154
  526.9 36.0 %fusion.173 = f32[32,1,16,1024]{3,2,1,0:T(8,128)S(1)} fusion(f32[32,1,16,1024]{3,2,1,0:T(8,128)S(1)} %bitcast.297, f32[]{:T(128)} %bitcast.50, f32[]{:T(128)} %bitcast.49, f32[]{:T(128)} %bitcast.48, f32[]{:T(128)} %bitcast.47, f32[]{:T(128)} %bitcast.46, f32[]{:T(128)} %bitcast.45, f32[]{:T(128)} %bitcast.44, f32[]{:T(128)} %bitcast.43, f32[]{:T(128)} %bitcast.42, ...), kind=kLoop, calls=%fused_computation.299 | loop fusion | flops 31981568 | bytes 4194428 | tf_op jit(solution)/shard_map/add | solution.py:32
  562.9 30.6 %all_to_all.191 = f32[32,1,16,1024]{3,2,1,0:T(8,128)} all-to-all(f32[32,1,16,1024]{3,2,1,0:T(8,128)S(1)} %fusion.173), channel_id=1, replica_groups=mesh['scan'=16,'row'=8] {'scan'}, dimensions={0} | all-to-all | bytes 4194304 | tf_op jit(solution)/shard_map/all_to_all | solution.py:54
  593.5 21.4 %copy.111 = f32[2,16,16,1024]{2,0,1,3:T(2,128)} copy(f32[2,16,16,1024]{3,2,0,1:T(8,128)} %bitcast.294) | data formatting | bytes 4194304 | tf_op jit(solution)/shard_map/all_to_all | solution.py:54
  614.9 24.7 %reshape.190 = f32[8,1,65536]{2,1,0:T(1,128)} reshape(f32[1024,16,2,16]{3,2,1,0:T(2,128)} %bitcast.285) | data formatting | bytes 4194304
  639.7 32.8 %all_to_all.192 = f32[8,1,65536]{2,1,0:T(1,128)} all-to-all(f32[8,1,65536]{2,1,0:T(1,128)} %reshape.190), channel_id=1, replica_groups=mesh['scan'=16,'row'=8] {'row'}, dimensions={0} | all-to-all | bytes 4194304 | tf_op jit(solution)/shard_map/all_to_all | solution.py:53
  672.5 8.6 reduce.4
  681.1 31.8 %reshape.191 = f32[1024,16,2,16]{3,2,1,0:T(2,128)} reshape(f32[8,65536]{1,0:T(8,128)} %reduce.4) | data formatting | bytes 4194304
  712.9 21.6 %copy.133 = f32[2,16,16,8,128]{4,2,3,1,0:T(8,128)} copy(f32[2,16,16,8,128]{2,0,1,4,3:T(2,128)} %bitcast.286) | data formatting | bytes 4194304 | tf_op jit(solution)/shard_map/all_to_all | solution.py:53
  734.5 57.3 %bitcast_divide_fusion = f32[2,2048,128]{2,1,0:T(8,128)S(1)} fusion(f32[2,16,8,16,128]{4,3,2,1,0:T(8,128)S(1)} %copy.94, f32[2,2048,128]{2,1,0:T(8,128)} %bitcast.290, f32[]{:T(128)} %bitcast.88, f32[]{:T(128)} %bitcast.87, f32[]{:T(128)} %bitcast.86, f32[]{:T(128)} %bitcast.85, f32[]{:T(128)} %bitcast.84, f32[]{:T(128)} %bitcast.83, f32[]{:T(128)} %bitcast.82, ...), kind=kLoop, calls=%fused_computation.372 | loop fusion | flops 33030144 | bytes 6291580 | tf_op jit(solution)/shard_map/div | solution.py:96
  791.8 27.6 %multiply_add_fusion = f32[2,2048,128]{2,1,0:T(8,128)S(1)} fusion(f32[2,2048,128]{2,1,0:T(8,128)S(1)} %bitcast_divide_fusion, f32[]{:T(128)} %bitcast.118, f32[]{:T(128)} %bitcast.117, f32[]{:T(128)} %bitcast.116, f32[]{:T(128)} %bitcast.115, f32[]{:T(128)} %bitcast.114, f32[]{:T(128)} %bitcast.113, f32[]{:T(128)} %bitcast.112, f32[]{:T(128)} %bitcast.111, ...), kind=kLoop, calls=%fused_computation.377 | loop fusion | flops 31981568 | bytes 4194428 | tf_op jit(solution)/shard_map/add | solution.py:32
  819.6 29.8 %all_to_all.193 = f32[2,16,128,128]{3,2,0,1:T(8,128)S(1)} all-to-all(f32[2,16,128,128]{3,2,0,1:T(8,128)S(1)} %copy.114), channel_id=1, replica_groups=mesh['scan'=16,'row'=8] {'scan'}, dimensions={1} | all-to-all | bytes 4194304 | tf_op jit(solution)/shard_map/all_to_all | solution.py:65
  849.4 1.2 copy.115
  850.7 31.1 %all_to_all.194 = f32[32,1,128,128]{3,0,1,2:T(8,128)S(1)} all-to-all(f32[32,1,128,128]{3,0,1,2:T(8,128)S(1)} %copy.115), channel_id=1, replica_groups=mesh['scan'=16,'row'=8] {'row'}, dimensions={2} | all-to-all | bytes 4194304 | tf_op jit(solution)/shard_map/all_to_all | solution.py:64
  881.8 1.2 copy.116
  883.0 0.9 copy.117
  884.4 36.1 %fusion.233 = f32[32,1,16,1024]{3,2,1,0:T(8,128)S(1)} fusion(f32[32,1,16,1024]{3,2,1,0:T(8,128)S(1)} %copy.118, f32[]{:T(128)} %bitcast.155, f32[]{:T(128)} %bitcast.154, f32[]{:T(128)} %bitcast.153, f32[]{:T(128)} %bitcast.152, f32[]{:T(128)} %bitcast.151, f32[]{:T(128)} %bitcast.150, f32[]{:T(128)} %bitcast.149, f32[]{:T(128)} %bitcast.148, f32[]{:T(128)} %bitcast.147, ...), kind=kLoop, calls=%fused_computation.359 | loop fusion | flops 31981568 | bytes 4194428 | tf_op jit(solution)/shard_map/add | solution.py:32
  920.5 3.1 multiply_bitcast_fusion
  923.6 2.5 copy.122
  (53 shorter events, 13.5 us)
Async XLA Ops:
  0.0 3.2 copy-start.5
  0.0 3.2 copy-start.4
  20.8 8.8 copy-start.6
  20.8 9.6 %copy-start.8 = (f32[64]{0:T(128)S(1)}, f32[64]{0:T(128)}, u32[]{:S(2)}) copy-start(f32[64]{0:T(128)} %param.7) | copy-start | bytes 772
  20.8 39.3 %all-to-all-start = ((f32[2,16,16,1024]{3,2,0,1:T(8,128)}), f32[2,16,16,1024]{3,2,0,1:T(8,128)}, u32[]{:S(2)}, u32[]{:S(2)}) async-start(f32[2,16,16,1024]{3,2,0,1:T(8,128)} %get-tuple-element.10), calls=%async_computation | async-start | bytes 4194304 | tf_op jit(solution)/shard_map/all_to_all | solution.py:84
  61.9 1.3 copy-start.2
  133.6 50.2 %all-to-all-start.1 = ((f32[32,1,16,1024]{3,2,1,0:T(8,128)}), f32[32,1,16,1024]{3,2,1,0:T(8,128)S(1)}, u32[]{:S(2)}, u32[]{:S(2)}) async-start(f32[32,1,16,1024]{3,2,1,0:T(8,128)} %bitcast.9), calls=%async_computation.1 | async-start | bytes 4194304 | tf_op jit(solution)/shard_map/all_to_all | solution.py:54
  183.9 43.3 %all-to-all-start.4 = ((f32[8,1,65536]{2,1,0:T(1,128)}), f32[8,1,65536]{2,1,0:T(1,128)}, u32[]{:S(2)}, u32[]{:S(2)}) async-start(f32[8,1,65536]{2,1,0:T(1,128)} %reshape.188), calls=%async_computation.4 | async-start | bytes 4194304 | tf_op jit(solution)/shard_map/all_to_all | solution.py:53
  227.2 4.9 copy-start.7
  227.2 67.3 %all-to-all-start.2 = ((f32[8,1,65536]{2,1,0:T(1,128)}), f32[8,1,65536]{2,1,0:T(1,128)}, u32[]{:S(2)}, u32[]{:S(2)}) async-start(f32[8,1,65536]{2,1,0:T(1,128)} %reshape.186), calls=%async_computation.2 | async-start | bytes 4194304 | tf_op jit(solution)/shard_map/all_to_all | solution.py:53
  445.6 32.2 %all-to-all-start.6 = ((f32[32,1,128,128]{3,0,1,2:T(8,128)}), f32[32,1,128,128]{3,0,1,2:T(8,128)}, u32[]{:S(2)}, u32[]{:S(2)}) async-start(f32[32,1,128,128]{3,0,1,2:T(8,128)} %copy.101), calls=%async_computation.6 | async-start | bytes 4194304 | tf_op jit(solution)/shard_map/all_to_all | solution.py:64
  482.0 36.3 %copy-start.3 = (f32[16,2,1,16,1024]{4,3,1,0,2:T(8,128)S(1)}, f32[16,2,1,16,1024]{4,3,1,0,2:T(8,128)}, u32[]{:S(2)}) copy-start(f32[16,2,1,16,1024]{4,3,1,0,2:T(8,128)} %copy-done.2) | copy-start | bytes 6291460
  522.5 1.3 copy-start
  884.4 36.2 %copy-start.1 = (f32[32,16,1024]{2,0,1:T(8,128)S(1)}, f32[32,16,1024]{2,0,1:T(8,128)}, u32[]{:S(2)}) copy-start(f32[32,16,1024]{2,0,1:T(8,128)} %copy-done) | copy-start | bytes 6291460
where the time goes:
time: 942 us; the launch traced here: 927 us
  other arithmetic  357 us (38%)
  local copies, waits for them, and re-layouts  293 us (31%)
  blocking collectives  190 us (20%)
  waiting for transfers between devices  44.7 us (5%)
  starting transfers between devices  30.1 us (3%)
  matrix products  11 us (1%)
    add x6, other arithmetic, shifted_sum(): summed + kernel[tap] * lax.slice_in_dim(padded, tap, tap + extent, axis=a...  199 us
    unnamed x30, local copies, waits for them, and re-layouts  149 us
    div x2, other arithmetic, shards(): quotient = data_flat / (flattened + background_level)  115 us
    all_to_all x2, blocking collectives, pencil_layout(): lax.all_to_all(volume, 'scan', split_axis=1, concat_axis=0, tiled=True)  64.6 us
    all_to_all x2, blocking collectives, rows_layout(): lax.all_to_all(volume, 'scan', split_axis=0, concat_axis=1, tiled=True)  61.9 us
    all_to_all x3, local copies, waits for them, and re-layouts, rows_layout(): lax.all_to_all(volume, 'scan', split_axis=0, concat_axis=1, tiled=True)  56.4 us
    all_to_all x4, local copies, waits for them, and re-layouts, rows_layout(): lax.all_to_all(lax.all_to_all(volume, 'scan', split_axis=0, concat_axis=1...  53.8 us
    all_to_all x1, blocking collectives, rows_layout(): lax.all_to_all(lax.all_to_all(volume, 'scan', split_axis=0, concat_axis=1...  32.8 us
  transfers between devices with their start and end apart: 5, of which 2 were waited for; matrix products, arithmetic and copies ran while one was open for 17% of the time, Pallas kernels for 0%

commit v1 on v0

--- a/solution.py
+++ b/solution.py
@@ -50,12 +50,20 @@
 
 
 def rows_layout(volume):
-    result = lax.all_to_all(
-        lax.all_to_all(volume, "scan", split_axis=0, concat_axis=1, tiled=True),
-        "row",
-        split_axis=3,
-        concat_axis=2,
-        tiled=True,
+    result = jnp.concatenate(
+        lax.all_to_all(
+            jnp.stack(
+                jnp.split(
+                    lax.all_to_all(volume, "scan", split_axis=0, concat_axis=1, tiled=True),
+                    lax.axis_size("row"),
+                    axis=3,
+                )
+            ),
+            "row",
+            0,
+            0,
+        ),
+        axis=2,
     )
     return result
 

time: 942 us -> 682 us (0.72)
  local copies, waits for them, and re-layouts: 293 us -> 60.7 us
  other arithmetic: 357 us -> 281 us
  waiting for transfers between devices: 44.7 us -> 101 us
    unnamed x30 -> x46, local copies, waits for them, and re-layouts: 149 us -> 20 us
    all_to_all x7 -> x0, local copies, waits for them, and re-layouts: 110 us -> none  [the longest x3 56.4 us: rows_layout(): lax.all_to_all(volume, 'scan', split_axis=0, concat_axis=1, tiled=True)]
    div x2, other arithmetic: 115 us -> 55.3 us  [shards(): quotient = data_flat / (flattened + background_level)]
    all_to_all x2, waiting for transfers between devices: 0.01 us -> 39.3 us  [rows_layout(): lax.all_to_all(jnp.stack(jnp.split(lax.all_to_all(volume, 'scan', split_a...]
    all_to_all x3 -> x0, other arithmetic: 23.1 us -> none  [rows_layout(): lax.all_to_all(lax.all_to_all(volume, 'scan', split_axis=0, concat_axis=1...]
    all_to_all x1, waiting for transfers between devices: 0.01 us -> 16.4 us  [rows_layout(): lax.all_to_all(volume, 'scan', split_axis=0, concat_axis=1, tiled=True)]
  transfers between devices with their start and end apart: 5 -> 5, of which waited for: 2 -> 5; matrix products, arithmetic and copies ran while one was open for 17% -> 5% of each run, Pallas kernels for 0% -> 0%
where the time goes in v1:
time: 682 us; the launch traced here: 671 us
  other arithmetic  281 us (41%)
  blocking collectives  184 us (27%)
  waiting for transfers between devices  101 us (15%)
  local copies, waits for them, and re-layouts  60.7 us (9%)
  starting transfers between devices  32.7 us (5%)
  matrix products  11 us (2%)
    add x6, other arithmetic, shifted_sum(): summed + kernel[tap] * lax.slice_in_dim(padded, tap, tap + extent, axis=a...  207 us
    all_to_all x2, blocking collectives, rows_layout(): lax.all_to_all(volume, 'scan', split_axis=0, concat_axis=1, tiled=True)  61.2 us
    all_to_all x2, blocking collectives, pencil_layout(): lax.all_to_all(volume, 'scan', split_axis=1, concat_axis=0, tiled=True)  59.8 us
    div x2, other arithmetic, shards(): quotient = data_flat / (flattened + background_level)  55.3 us
    all_to_all x2, waiting for transfers between devices, rows_layout(): lax.all_to_all(jnp.stack(jnp.split(lax.all_to_all(volume, 'scan', split_a...  39.3 us
    all_to_all x1, blocking collectives, pencil_layout(): lax.all_to_all(lax.all_to_all(volume, 'scan', split_axis=1, concat_axis=0...  31.4 us
    all_to_all x1, blocking collectives, rows_layout(): lax.all_to_all(jnp.stack(jnp.split(lax.all_to_all(volume, 'scan', split_a...  31.2 us
    all_to_all x1, waiting for transfers between devices, pencil_layout(): lax.all_to_all(lax.all_to_all(volume, 'scan', split_axis=1, concat_axis=0...  25 us
  transfers between devices with their start and end apart: 5, of which 5 were waited for; matrix products, arithmetic and copies ran while one was open for 5% of the time, Pallas kernels for 0%

profile of v1, /device:TPU:1, one launch (start us, length us, event | category | flops | bytes accessed | tf_op | source)
XLA Modules:
  0.0 670.6 jit_solution(1431313124974799359)
XLA Ops:
  1.6 1.6 broadcast_in_dim.16.clone
  3.2 17.9 %while.1 = (s32[]{:T(128)}, f32[2,16,16,1024]{3,2,0,1:T(8,128)}, s32[2,4]{1,0:T(2,128)S(1)}, f32[2,6,16,1024]{3,2,1,0:T(8,128)S(1)}, s32[]{:T(128)}, /*index=5*/s32[4]{0:T(128)S(1)}) while((s32[]{:T(128)}, f32[2,16,16,1024]{3,2,0,1:T(8,128)}, s32[2,4]{1,0:T(2,128)S(1)}, f32[2,6,16,1024]{3,2,1,0:T(8,128)S(1)}, s32[]{:T(128)}, ...), condition=%wide.while_cond, body=%wide.while_body.sunk | while | flops 98333 | bytes 1968306 | solution.py:41
  3.8 3.3 and_reduce_fusion.2
  7.1 2.3 constant_dynamic-slice_fusion.5
  9.4 2.7 bitcast_dynamic-update-slice_fusion.2
  12.8 3.3 and_reduce_fusion.2
  16.1 2.3 constant_dynamic-slice_fusion.5
  18.3 2.7 bitcast_dynamic-update-slice_fusion.2
  21.1 8.8 %all-to-all-start = ((f32[2,16,16,1024]{3,2,0,1:T(8,128)}), f32[2,16,16,1024]{3,2,0,1:T(8,128)}, u32[]{:S(2)}, u32[]{:S(2)}) async-start(f32[2,16,16,1024]{3,2,0,1:T(8,128)} %get-tuple-element.10), calls=%async_computation | async-start | bytes 4194304 | tf_op jit(solution)/shard_map/all_to_all | solution.py:92
  31.9 6.6 gather_fusion
  40.6 19.8 %all-to-all-done = f32[2,16,16,1024]{3,2,0,1:T(8,128)} async-done(((f32[2,16,16,1024]{3,2,0,1:T(8,128)}), f32[2,16,16,1024]{3,2,0,1:T(8,128)}, u32[]{:S(2)}, u32[]{:S(2)}) %all-to-all-start) | async-done | bytes 2097184 | tf_op jit(solution)/shard_map/all_to_all | solution.py:92
  60.4 1.9 bitcast_add_fusion
  62.3 1.2 copy.133
  63.6 1.9 fusion.353
  65.6 1.2 copy.134
  66.8 35.8 %fusion.53 = f32[32,1,16,1024]{3,2,1,0:T(8,128)S(1)} fusion(f32[32,1,16,1024]{3,2,1,0:T(8,128)S(1)} %bitcast.396, f32[]{:T(128)} %bitcast.58, f32[]{:T(128)} %bitcast.57, f32[]{:T(128)} %bitcast.56, f32[]{:T(128)} %bitcast.55, f32[]{:T(128)} %bitcast.54, f32[]{:T(128)} %bitcast.53, f32[]{:T(128)} %bitcast.52, f32[]{:T(128)} %bitcast.51, f32[]{:T(128)} %bitcast.50, ...), kind=kLoop, calls=%fused_computation.179 | loop fusion | flops 31981568 | bytes 4194428 | tf_op jit(solution)/shard_map/add | solution.py:32
  102.6 31.3 %all_to_all.159 = f32[32,1,16,1024]{3,2,1,0:T(8,128)} all-to-all(f32[32,1,16,1024]{3,2,1,0:T(8,128)S(1)} %fusion.53), channel_id=1, replica_groups=mesh['scan'=16,'row'=8] {'scan'}, dimensions={0} | all-to-all | bytes 4194304 | tf_op jit(solution)/shard_map/all_to_all | solution.py:57
  133.8 3.7 all-to-all-start.1
  137.6 1.8 fusion.333
  139.4 1.7 fusion.332
  141.1 1.7 fusion.331
  142.8 1.7 fusion.330
  145.9 0.8 fusion.327
  146.7 0.8 fusion.326
  147.4 16.4 %all-to-all-done.1 = f32[32,1,16,1024]{3,2,1,0:T(8,128)S(1)} async-done(((f32[32,1,16,1024]{3,2,1,0:T(8,128)}), f32[32,1,16,1024]{3,2,1,0:T(8,128)S(1)}, u32[]{:S(2)}, u32[]{:S(2)}) %all-to-all-start.1) | async-done | bytes 2097184 | tf_op jit(solution)/shard_map/all_to_all | solution.py:57
  163.9 9.4 %all-to-all-start.4 = ((f32[8,2,16,16,128]{4,3,1,2,0:T(8,128)}), f32[8,2,16,16,128]{4,3,1,2,0:T(8,128)}, u32[]{:S(2)}, u32[]{:S(2)}) async-start(f32[8,2,16,16,128]{4,3,1,2,0:T(8,128)} %fusion.326), calls=%async_computation.4 | async-start | bytes 4194304 | tf_op jit(solution)/shard_map/all_to_all | solution.py:54
  174.0 0.7 fusion.340
  174.7 0.7 fusion.339
  175.5 0.8 fusion.338
  176.2 0.8 fusion.337
  177.0 0.8 fusion.336
  177.7 0.8 fusion.335
  178.5 0.8 fusion.334
  179.3 20.4 %all-to-all-done.4 = f32[8,2,16,16,128]{4,3,1,2,0:T(8,128)} async-done(((f32[8,2,16,16,128]{4,3,1,2,0:T(8,128)}), f32[8,2,16,16,128]{4,3,1,2,0:T(8,128)}, u32[]{:S(2)}, u32[]{:S(2)}) %all-to-all-start.4) | async-done | bytes 2097184 | tf_op jit(solution)/shard_map/all_to_all | solution.py:54
  199.7 4.7 all-to-all-start.2
  208.6 3.2 copy.89
  211.8 18.9 %all-to-all-done.2 = f32[8,2,16,16,128]{4,3,1,2,0:T(8,128)S(1)} async-done(((f32[8,2,16,16,128]{4,3,1,2,0:T(8,128)}), f32[8,2,16,16,128]{4,3,1,2,0:T(8,128)S(1)}, u32[]{:S(2)}, u32[]{:S(2)}) %all-to-all-start.2) | async-done | bytes 2097184 | tf_op jit(solution)/shard_map/all_to_all | solution.py:54
  230.7 1.3 copy-done.4
  232.0 2.0 copy.86
  234.2 27.6 %bitcast_divide_fusion.1 = f32[2,2048,128]{2,1,0:T(8,128)S(1)} fusion(f32[2,16,8,16,128]{4,3,2,1,0:T(8,128)S(1)} %copy.86, f32[2,2048,128]{2,1,0:T(8,128)S(1)} %bitcast.390, f32[]{:T(128)} %bitcast.103, f32[]{:T(128)} %bitcast.102, f32[]{:T(128)} %bitcast.101, f32[]{:T(128)} %bitcast.100, f32[]{:T(128)} %bitcast.99, f32[]{:T(128)} %bitcast.98, f32[]{:T(128)} %bitcast.97, ...), kind=kLoop, calls=%fused_computation.373 | loop fusion | flops 33030144 | bytes 6291580 | tf_op jit(solution)/shard_map/div | solution.py:104
  261.8 27.3 %multiply_add_fusion.1 = f32[2,2048,128]{2,1,0:T(8,128)S(1)} fusion(f32[2,2048,128]{2,1,0:T(8,128)S(1)} %bitcast_divide_fusion.1, f32[]{:T(128)} %bitcast.133, f32[]{:T(128)} %bitcast.132, f32[]{:T(128)} %bitcast.131, f32[]{:T(128)} %bitcast.130, f32[]{:T(128)} %bitcast.129, f32[]{:T(128)} %bitcast.128, f32[]{:T(128)} %bitcast.127, f32[]{:T(128)} %bitcast.126, ...), kind=kLoop, calls=%fused_computation.430 | loop fusion | flops 31981568 | bytes 4194428 | tf_op jit(solution)/shard_map/add | solution.py:32
  289.4 30.0 %all_to_all.160 = f32[2,16,128,128]{3,2,0,1:T(8,128)S(1)} all-to-all(f32[2,16,128,128]{3,2,0,1:T(8,128)S(1)} %copy.90), channel_id=1, replica_groups=mesh['scan'=16,'row'=8] {'scan'}, dimensions={1} | all-to-all | bytes 4194304 | tf_op jit(solution)/shard_map/all_to_all | solution.py:73
  319.4 2.6 copy.91
  322.0 6.2 all-to-all-start.6
  329.6 25.0 %all-to-all-done.6 = f32[32,1,128,128]{3,0,1,2:T(8,128)} async-done(((f32[32,1,128,128]{3,0,1,2:T(8,128)}), f32[32,1,128,128]{3,0,1,2:T(8,128)}, u32[]{:S(2)}, u32[]{:S(2)}) %all-to-all-start.6) | async-done | bytes 2097184 | tf_op jit(solution)/shard_map/all_to_all | solution.py:72
  354.6 2.8 copy.92
  357.5 0.9 copy.93
  358.8 44.8 %fusion.113 = f32[32,1,16,1024]{3,2,1,0:T(8,128)S(1)} fusion(f32[32,1,16,1024]{3,2,1,0:T(8,128)S(1)} %copy.94, f32[]{:T(128)} %bitcast.170, f32[]{:T(128)} %bitcast.169, f32[]{:T(128)} %bitcast.168, f32[]{:T(128)} %bitcast.167, f32[]{:T(128)} %bitcast.166, f32[]{:T(128)} %bitcast.165, f32[]{:T(128)} %bitcast.164, f32[]{:T(128)} %bitcast.163, f32[]{:T(128)} %bitcast.162, ...), kind=kLoop, calls=%fused_computation.239 | loop fusion | flops 31981568 | bytes 4194428 | tf_op jit(solution)/shard_map/add | solution.py:32
  403.6 4.1 copy_multiply_fusion
  407.9 1.9 fusion.350
  409.8 1.2 copy.136
  411.1 35.8 %fusion.173 = f32[32,1,16,1024]{3,2,1,0:T(8,128)S(1)} fusion(f32[32,1,16,1024]{3,2,1,0:T(8,128)S(1)} %bitcast.394, f32[]{:T(128)} %bitcast.58, f32[]{:T(128)} %bitcast.57, f32[]{:T(128)} %bitcast.56, f32[]{:T(128)} %bitcast.55, f32[]{:T(128)} %bitcast.54, f32[]{:T(128)} %bitcast.53, f32[]{:T(128)} %bitcast.52, f32[]{:T(128)} %bitcast.51, f32[]{:T(128)} %bitcast.50, ...), kind=kLoop, calls=%fused_computation.299 | loop fusion | flops 31981568 | bytes 4194428 | tf_op jit(solution)/shard_map/add | solution.py:32
  446.9 30.0 %all_to_all.161 = f32[32,1,16,1024]{3,2,1,0:T(8,128)S(1)} all-to-all(f32[32,1,16,1024]{3,2,1,0:T(8,128)S(1)} %fusion.173), channel_id=1, replica_groups=mesh['scan'=16,'row'=8] {'scan'}, dimensions={0} | all-to-all | bytes 4194304 | tf_op jit(solution)/shard_map/all_to_all | solution.py:57
  477.2 31.2 %all_to_all.162 = f32[8,2,16,16,128]{4,3,1,2,0:T(8,128)S(1)} all-to-all(f32[8,2,16,16,128]{4,3,1,2,0:T(8,128)S(1)} %fusion.318), channel_id=1, replica_groups=mesh['scan'=16,'row'=8] {'row'}, dimensions={0} | all-to-all | bytes 4194304 | tf_op jit(solution)/shard_map/all_to_all | solution.py:54
  508.6 27.6 %bitcast_divide_fusion = f32[2,2048,128]{2,1,0:T(8,128)S(1)} fusion(f32[2,16,8,16,128]{4,3,2,1,0:T(8,128)S(1)} %copy.86, f32[2,2048,128]{2,1,0:T(8,128)S(1)} %bitcast.373, f32[]{:T(128)} %bitcast.103, f32[]{:T(128)} %bitcast.102, f32[]{:T(128)} %bitcast.101, f32[]{:T(128)} %bitcast.100, f32[]{:T(128)} %bitcast.99, f32[]{:T(128)} %bitcast.98, f32[]{:T(128)} %bitcast.97, ...), kind=kLoop, calls=%fused_computation.372 | loop fusion | flops 33030144 | bytes 6291580 | tf_op jit(solution)/shard_map/div | solution.py:104
  536.2 27.3 %multiply_add_fusion = f32[2,2048,128]{2,1,0:T(8,128)S(1)} fusion(f32[2,2048,128]{2,1,0:T(8,128)S(1)} %bitcast_divide_fusion, f32[]{:T(128)} %bitcast.133, f32[]{:T(128)} %bitcast.132, f32[]{:T(128)} %bitcast.131, f32[]{:T(128)} %bitcast.130, f32[]{:T(128)} %bitcast.129, f32[]{:T(128)} %bitcast.128, f32[]{:T(128)} %bitcast.127, f32[]{:T(128)} %bitcast.126, ...), kind=kLoop, calls=%fused_computation.377 | loop fusion | flops 31981568 | bytes 4194428 | tf_op jit(solution)/shard_map/add | solution.py:32
  563.7 29.8 %all_to_all.163 = f32[2,16,128,128]{3,2,0,1:T(8,128)S(1)} all-to-all(f32[2,16,128,128]{3,2,0,1:T(8,128)S(1)} %copy.102), channel_id=1, replica_groups=mesh['scan'=16,'row'=8] {'scan'}, dimensions={1} | all-to-all | bytes 4194304 | tf_op jit(solution)/shard_map/all_to_all | solution.py:73
  593.5 1.2 copy.103
  594.7 31.4 %all_to_all.164 = f32[32,1,128,128]{3,0,1,2:T(8,128)S(1)} all-to-all(f32[32,1,128,128]{3,0,1,2:T(8,128)S(1)} %copy.103), channel_id=1, replica_groups=mesh['scan'=16,'row'=8] {'row'}, dimensions={2} | all-to-all | bytes 4194304 | tf_op jit(solution)/shard_map/all_to_all | solution.py:72
  626.1 1.2 copy.104
  627.3 0.9 copy.105
  628.7 35.9 %fusion.233 = f32[32,1,16,1024]{3,2,1,0:T(8,128)S(1)} fusion(f32[32,1,16,1024]{3,2,1,0:T(8,128)S(1)} %copy.106, f32[]{:T(128)} %bitcast.170, f32[]{:T(128)} %bitcast.169, f32[]{:T(128)} %bitcast.168, f32[]{:T(128)} %bitcast.167, f32[]{:T(128)} %bitcast.166, f32[]{:T(128)} %bitcast.165, f32[]{:T(128)} %bitcast.164, f32[]{:T(128)} %bitcast.163, f32[]{:T(128)} %bitcast.162, ...), kind=kLoop, calls=%fused_computation.359 | loop fusion | flops 31981568 | bytes 4194428 | tf_op jit(solution)/shard_map/add | solution.py:32
  664.6 3.1 multiply_bitcast_fusion
  667.6 2.5 copy.110
  (65 shorter events, 17.1 us)
Async XLA Ops:
  0.0 3.2 copy-start.6
  0.0 3.2 copy-start.5
  21.1 8.8 %copy-start.7 = (f32[31]{0:T(128)S(1)}, f32[31]{0:T(128)}, u32[]{:S(2)}) copy-start(f32[31]{0:T(128)} %param.8) | copy-start | bytes 376
  21.1 9.6 %copy-start.9 = (f32[64]{0:T(128)S(1)}, f32[64]{0:T(128)}, u32[]{:S(2)}) copy-start(f32[64]{0:T(128)} %param.7) | copy-start | bytes 772
  21.1 39.3 %all-to-all-start = ((f32[2,16,16,1024]{3,2,0,1:T(8,128)}), f32[2,16,16,1024]{3,2,0,1:T(8,128)}, u32[]{:S(2)}, u32[]{:S(2)}) async-start(f32[2,16,16,1024]{3,2,0,1:T(8,128)} %get-tuple-element.10), calls=%async_computation | async-start | bytes 4194304 | tf_op jit(solution)/shard_map/all_to_all | solution.py:92
  62.3 1.3 copy-start
  133.8 30.0 %all-to-all-start.1 = ((f32[32,1,16,1024]{3,2,1,0:T(8,128)}), f32[32,1,16,1024]{3,2,1,0:T(8,128)S(1)}, u32[]{:S(2)}, u32[]{:S(2)}) async-start(f32[32,1,16,1024]{3,2,1,0:T(8,128)} %bitcast.9), calls=%async_computation.1 | async-start | bytes 4194304 | tf_op jit(solution)/shard_map/all_to_all | solution.py:57
  137.6 6.9 %copy-start.2 = (f32[32,1,16,1024]{3,2,1,0:T(8,128)S(1)}, f32[32,1,16,1024]{3,2,1,0:T(8,128)}, u32[]{:S(2)}) copy-start(f32[32,1,16,1024]{3,2,1,0:T(8,128)} %all_to_all.159) | copy-start | bytes 6291460
  163.9 35.8 %all-to-all-start.4 = ((f32[8,2,16,16,128]{4,3,1,2,0:T(8,128)}), f32[8,2,16,16,128]{4,3,1,2,0:T(8,128)}, u32[]{:S(2)}, u32[]{:S(2)}) async-start(f32[8,2,16,16,128]{4,3,1,2,0:T(8,128)} %fusion.326), calls=%async_computation.4 | async-start | bytes 4194304 | tf_op jit(solution)/shard_map/all_to_all | solution.py:54
  179.3 25.1 %copy-start.8 = (f32[31]{0:T(128)S(1)}, f32[31]{0:T(128)}, u32[]{:S(2)}) copy-start(f32[31]{0:T(128)} %param.9) | copy-start | bytes 376
  199.7 31.0 %all-to-all-start.2 = ((f32[8,2,16,16,128]{4,3,1,2,0:T(8,128)}), f32[8,2,16,16,128]{4,3,1,2,0:T(8,128)S(1)}, u32[]{:S(2)}, u32[]{:S(2)}) async-start(f32[8,2,16,16,128]{4,3,1,2,0:T(8,128)} %fusion.334), calls=%async_computation.2 | async-start | bytes 4194304 | tf_op jit(solution)/shard_map/all_to_all | solution.py:54
  230.7 1.3 copy-start.4
  232.0 2.2 copy-start.3
  322.0 32.7 %all-to-all-start.6 = ((f32[32,1,128,128]{3,0,1,2:T(8,128)}), f32[32,1,128,128]{3,0,1,2:T(8,128)}, u32[]{:S(2)}, u32[]{:S(2)}) async-start(f32[32,1,128,128]{3,0,1,2:T(8,128)} %copy.91), calls=%async_computation.6 | async-start | bytes 4194304 | tf_op jit(solution)/shard_map/all_to_all | solution.py:72
  358.8 44.8 %copy-start.1 = (f32[16,2,1,16,1024]{4,3,1,0,2:T(8,128)S(1)}, f32[16,2,1,16,1024]{4,3,1,0,2:T(8,128)}, u32[]{:S(2)}) copy-start(f32[16,2,1,16,1024]{4,3,1,0,2:T(8,128)} %copy-done) | copy-start | bytes 6291460
